TPU v7x, 32 devices: a whole 2x2x4 slice. The times are simulated.
32 devices in a mesh: gx: 4 (over y, x), gy: 8 (over z, core).
Axes of the slice: x: 2, y: 2, z: 4, core: 2. Of those that a mesh axis runs over, the one named last changes fastest.
Arguments:
- dist_start: float32 [19, 2, 512, 1024], P(None, None, 'gx', 'gy'), may hold values from -6 to 6
- cotangent: float32 [19, 2, 512, 1024], P(None, None, 'gx', 'gy'), may hold values from -6 to 6
- solid_mask: int32 [2, 512, 1024], P(None, 'gx', 'gy'), may hold values 0 or 1
- weight_in: bfloat16 [19, 128], replicated, may hold values from -1.25 to 1.25
- bias_in: float32 [128], replicated, may hold values from -3 to 3
- weight_out: bfloat16 [128, 19], replicated, may hold values from -0.5 to 0.5
- bias_out: float32 [19], replicated, may hold values from -3 to 3
Outputs:
- grad_start: float32 [19, 2, 512, 1024], P(None, None, 'gx', 'gy')
- grad_weight_in: float32 [19, 128], replicated
- grad_bias_in: float32 [128], replicated
- grad_weight_out: float32 [128, 19], replicated
- grad_bias_out: float32 [19], replicated
Inputs may be any that keep to these rules, and one draw needn't show every extreme that they name: `solid_mask`: 1 marks a solid cell.
All inputs are finite; a program needn't handle non-finite values. No bound on the sum of `solid_mask` on one device may be relied on, other than what follows from the above.
Results may differ from a plain program's by a relative error of at most 0.0067.
Values may be sent and summed in bfloat16 or wider, within the bound.
A program may use at most 256 MiB of HBM per device.

v0:
```python
import functools
import math

import jax
import jax.numpy as jnp
import numpy as np
from jax import lax
from jax.experimental import pallas as pl
from jax.experimental.pallas import tpu as pltpu
from jax.sharding import PartitionSpec as P

velocities = (
    (0, 0, 0),
    (1, 0, 0),
    (-1, 0, 0),
    (0, 1, 0),
    (0, -1, 0),
    (0, 0, 1),
    (0, 0, -1),
    (1, 1, 0),
    (-1, -1, 0),
    (1, -1, 0),
    (-1, 1, 0),
    (1, 0, 1),
    (-1, 0, -1),
    (1, 0, -1),
    (-1, 0, 1),
    (0, 1, 1),
    (0, -1, -1),
    (0, 1, -1),
    (0, -1, 1),
)
opposite = (0, 2, 1, 4, 3, 6, 5, 8, 7, 10, 9, 12, 11, 14, 13, 16, 15, 18, 17)
Q = 19
T = 8
KQ = Q * T
KA = KQ + 24
PAD = 8

PLUS_X = tuple(q for q in range(Q) if velocities[q][0] == 1)
MINUS_X = tuple(q for q in range(Q) if velocities[q][0] == -1)
REST = tuple(q for q in range(Q) if velocities[q][0] == 0)
SLOT = {q: s for s, q in enumerate(PLUS_X + MINUS_X + REST)}
NX5 = len(PLUS_X)
SIDE_Y = {
    1: tuple(q for q in range(Q) if velocities[q][1] == 1),
    -1: tuple(q for q in range(Q) if velocities[q][1] == -1),
}
MESH = pl.DeviceIdType.MESH


def kernel(
    nx,
    ny,
    factor,
    dist,
    cot,
    solid,
    first_in,
    first_out,
    second_out,
    second_in,
    bias_out,
    grad_start,
    sums,
    post_f,
    cot_f,
    mid_f,
    edge,
    halo,
    saved,
    a_in,
    a_out,
    b_out,
    b_in,
    act_s,
    hid_s,
    acc_in,
    acc_out,
    acc_bias,
    part_x,
    part_y,
    all_x,
    all_y,
    send_sem,
    recv_sem,
    sx_sem,
    rx_sem,
    sy_sem,
    ry_sem,
):
    me_x, me_y = lax.axis_index("gx"), lax.axis_index("gy")
    rows = dist.shape[2]
    tiles = rows // T
    H = first_in.shape[0]
    lanes = dist.shape[3]
    right_x, left_x = lax.rem(me_x + 1, nx), lax.rem(me_x + nx - 1, nx)
    right_y, left_y = lax.rem(me_y + 1, ny), lax.rem(me_y + ny - 1, ny)

    barrier = pltpu.get_barrier_semaphore()
    others = [(lax.rem(me_x + d, nx), me_y) for d in range(1, nx)]
    others += [(me_x, lax.rem(me_y + d, ny)) for d in range(1, ny)]
    others += [(a, b) for a in (left_x, right_x) for b in (left_y, right_y)]
    for other in others:
        pl.semaphore_signal(barrier, inc=1, device_id=other, device_id_type=MESH)

    col = lax.broadcasted_iota(jnp.int32, (H, KA), 1)
    row = lax.broadcasted_iota(jnp.int32, (KQ, H), 0)
    for s in range(T):
        keep = (col >= KQ) | ((col & (T - 1)) == s)
        a_in[s * H : (s + 1) * H, :] = jnp.where(keep, first_in[...], 0.0).astype(jnp.bfloat16)
        a_out[s * H : (s + 1) * H, :] = jnp.where(keep, first_out[...], 0.0).astype(jnp.bfloat16)
        mine = (row & (T - 1)) == s
        b_out[:, s * H : (s + 1) * H] = jnp.where(mine, second_out[...], 0.0).astype(jnp.bfloat16)
        b_in[:, s * H : (s + 1) * H] = jnp.where(mine, second_in[...], 0.0).astype(jnp.bfloat16)
    acc_in[...] = jnp.zeros_like(acc_in)
    acc_out[...] = jnp.zeros_like(acc_out)
    acc_bias[...] = jnp.zeros_like(acc_bias)

    lane = lax.broadcasted_iota(jnp.int32, (T, lanes), 1)

    def both(read):
        return jnp.concatenate([read(0), read(1)], axis=1)

    def widen(pieces, ones):
        tail = [jnp.full((T, 2 * lanes), ones, jnp.float32), jnp.zeros((2 * T, 2 * lanes), jnp.float32)]
        return jnp.concatenate(list(pieces) + tail, axis=0).astype(jnp.bfloat16)

    def put(field, number, orient, i, values):
        begin = pl.multiple_of(i * T, T)
        for q in range(Q):
            for z in range(2):
                field[SLOT[q], z, pl.ds(begin + PAD, T), :] = values[q][:, z * lanes : (z + 1) * lanes]
        for side in range(2):
            step = 1 - 2 * side
            columns = jnp.zeros((T, lanes), jnp.float32)
            for k, q in enumerate(SIDE_Y[orient * step]):
                for z in range(2):
                    at = z * lanes + (lanes - 1 if step == 1 else 0)
                    columns = jnp.where(lane == 2 * k + z, values[q][:, at : at + 1], columns)
            edge[number, side, pl.ds(begin, T), :] = columns

    def copies(field, number, orient):
        high, low = (0, NX5) if orient == 1 else (NX5, 0)
        last = rows + PAD
        pairs = [
            (field.at[pl.ds(high, NX5), :, pl.ds(rows, PAD), :], field.at[pl.ds(high, NX5), :, pl.ds(0, PAD), :], (right_x, me_y)),
            (field.at[pl.ds(low, NX5), :, pl.ds(PAD, PAD), :], field.at[pl.ds(low, NX5), :, pl.ds(last, PAD), :], (left_x, me_y)),
        ]
        for side, target in ((0, right_y), (1, left_y)):
            source, sink = edge.at[number, side], halo.at[number, side]
            pairs += [
                (source, sink.at[pl.ds(PAD, rows), :], (me_x, target)),
                (source.at[pl.ds(rows - PAD, PAD), :], sink.at[pl.ds(0, PAD), :], (right_x, target)),
                (source.at[pl.ds(0, PAD), :], sink.at[pl.ds(last, PAD), :], (left_x, target)),
            ]
        return [
            pltpu.make_async_remote_copy(
                src_ref=source,
                dst_ref=sink,
                send_sem=send_sem.at[number, n],
                recv_sem=recv_sem.at[number, n],
                device_id=target,
                device_id_type=MESH,
            )
            for n, (source, sink, target) in enumerate(pairs)
        ]

    def running(field, number, orient, i):
        pieces = []
        for q in range(Q):
            move_x, move_y, move_z = velocities[q]
            begin = i * T + PAD - orient * move_x
            if move_x == 0:
                begin = pl.multiple_of(begin, T)
            step = orient * move_y
            halves = []
            for z in range(2):
                from_z = (z + move_z) % 2
                tile = field[SLOT[q], from_z, pl.ds(begin, T), :]
                if step:
                    side = 0 if step == 1 else 1
                    k = 2 * SIDE_Y[move_y].index(q) + from_z
                    columns = halo[number, side, pl.ds(begin, T), :]
                    tile = pltpu.roll(tile, 1 if step == 1 else lanes - 1, 1)
                    tile = jnp.where(lane == (0 if step == 1 else lanes - 1), columns[:, k : k + 1], tile)
                halves.append(tile)
            pieces.append(jnp.concatenate(halves, axis=1))
        return pieces

    def own(i):
        begin = pl.multiple_of(i * T, T)
        return [both(lambda z: dist[q, z, pl.ds(begin, T), :]) for q in range(Q)]

    def solid_of(i):
        begin = pl.multiple_of(i * T, T)
        return both(lambda z: solid[z, pl.ds(begin, T), :]) > 0

    CH = 2 * H

    def dot(a, b):
        return jnp.dot(a, b, preferred_element_type=jnp.float32)

    def dot_t(a, b):
        return lax.dot_general(a, b, (((1,), (1,)), ((), ())), preferred_element_type=jnp.float32)

    def take(i, carry):
        begin = pl.multiple_of(i * T, T)
        put(cot_f, 0, -1, i, [both(lambda z: cot[q, z, pl.ds(begin, T), :]) for q in range(Q)])
        return carry

    lax.fori_loop(0, tiles, take, 0)
    pl.semaphore_wait(barrier, len(others))
    first = copies(cot_f, 0, -1)
    for copy in first:
        copy.start()

    def collide(i, carry):
        field = own(i)
        wide = widen(field, 1.0)
        for c in range(T * H // CH):
            part = slice(c * CH, (c + 1) * CH)
            saved[i, part, :] = jnp.tanh(dot(a_in[part, :], wide)).astype(jnp.bfloat16)
        out = dot(b_out[...], saved[i])
        is_solid = solid_of(i)
        posts = []
        for q in range(Q):
            at = slice(q * T, (q + 1) * T)
            value = field[q] + (out[at] + bias_out[at, :])
            value = jnp.where(is_solid, field[opposite[q]], value)
            posts.append(value.astype(jnp.bfloat16).astype(jnp.float32))
        put(post_f, 1, 1, i, posts)
        return carry

    lax.fori_loop(0, tiles, collide, 0)
    second = copies(post_f, 1, 1)
    for copy in second:
        copy.start()
    for copy in first + second:
        copy.wait()

    def backward(i, wide, grad, act_of):
        is_solid = solid_of(i)
        masked = [jnp.where(is_solid, 0.0, g) for g in grad]
        wide_out = widen(masked, 0.0)
        for c in range(T * H // CH):
            part = slice(c * CH, (c + 1) * CH)
            t = act_of(part)
            hid = dot(a_out[part, :], wide_out) * (1.0 - t * t)
            hid = hid.astype(jnp.bfloat16)
            hid_s[part, :] = hid
            acc_in[:, part] += dot_t(wide, hid)
        into = dot(b_in[...], hid_s[...])
        results = []
        for q in range(Q):
            at = slice(q * T, (q + 1) * T)
            acc_bias[at, :] += masked[q]
            results.append(masked[q] + into[at] + jnp.where(is_solid, grad[opposite[q]], 0.0))
        return wide_out, results

    def late(i, carry):
        wide = widen(running(post_f, 1, 1, i), 1.0)

        def act_of(part):
            t = jnp.tanh(dot(a_in[part, :], wide))
            act_s[part, :] = t.astype(jnp.bfloat16)
            return t

        wide_out, results = backward(i, wide, running(cot_f, 0, -1, i), act_of)
        for c in range(T * H // CH):
            part = slice(c * CH, (c + 1) * CH)
            acc_out[:, part] += dot_t(wide_out, act_s[part, :])
        put(mid_f, 2, -1, i, results)
        return carry

    lax.fori_loop(0, tiles, late, 0)
    third = copies(mid_f, 2, -1)
    for copy in third:
        copy.start()
    for copy in third:
        copy.wait()

    def early(i, carry):
        wide = widen(own(i), 1.0)
        wide_out, results = backward(
            i, wide, running(mid_f, 2, -1, i), lambda part: saved[i, part, :].astype(jnp.float32)
        )
        for c in range(T * H // CH):
            part = slice(c * CH, (c + 1) * CH)
            acc_out[:, part] += dot_t(wide_out, saved[i, part, :])
        begin = pl.multiple_of(i * T, T)
        for q in range(Q):
            for z in range(2):
                grad_start[q, z, pl.ds(begin, T), :] = results[q][:, z * lanes : (z + 1) * lanes]
        return carry

    lax.fori_loop(0, tiles, early, 0)

    tall = lax.broadcasted_iota(jnp.int32, (KA, H), 0) & (T - 1)

    def diagonal(acc):
        total = jnp.zeros((KA, H), jnp.float32)
        for s in range(T):
            total += jnp.where(tall == s, acc[:, s * H : (s + 1) * H], 0.0)
        return jnp.sum(total.reshape(KA // T, T, H), axis=1)

    part_x[...] = jnp.zeros_like(part_x)
    part_x[0 : KA // T, :] = diagonal(acc_in)
    part_x[24 : 24 + KA // T, :] = diagonal(acc_out)
    bias = jnp.sum(acc_bias[...], axis=1, keepdims=True)
    bias = jnp.broadcast_to(bias, (KQ, H)).reshape(Q, T, H)
    part_x[48 : 48 + Q, :] = jnp.sum(bias, axis=1)

    def gather(part, everyone, size, me, place, s_sem, r_sem):
        sends = [
            pltpu.make_async_remote_copy(
                src_ref=part,
                dst_ref=everyone.at[me],
                send_sem=s_sem.at[d - 1],
                recv_sem=r_sem.at[d - 1],
                device_id=place(lax.rem(me + d, size)),
                device_id_type=MESH,
            )
            for d in range(1, size)
        ]
        for copy in sends:
            copy.start()
        everyone[me] = part[...]
        for copy in sends:
            copy.wait()
        total = everyone[0]
        for d in range(1, size):
            total = total + everyone[d]
        return total

    part_y[...] = gather(part_x, all_x, nx, me_x, lambda a: (a, me_y), sx_sem, rx_sem)
    sums[...] = gather(part_y, all_y, ny, me_y, lambda b: (me_x, b), sy_sem, ry_sem) * factor


def shards(dist_start, cotangent, solid_mask, weight_in, bias_in, weight_out, bias_out):
    nx, ny = lax.axis_size("gx"), lax.axis_size("gy")
    H = weight_in.shape[1]
    rows, lanes = dist_start.shape[2:]
    tiles = rows // T
    f32, bf16 = jnp.float32, jnp.bfloat16
    factor = 1.0 / math.sqrt(solid_mask.size * nx * ny)

    def top(x):
        return lax.reduce_precision(x, 8, 7)

    one = top(bias_in)
    two = top(bias_in - one)
    three = top(bias_in - one - two)
    biases = jnp.stack([one, two, three], axis=1)
    w_in, w_out = weight_in.astype(f32), weight_out.astype(f32)
    first_in = jnp.concatenate(
        [jnp.repeat(w_in.T, T, axis=1), biases, jnp.zeros((H, KA - KQ - 3), f32)], axis=1
    )
    first_out = jnp.concatenate([jnp.repeat(w_out, T, axis=1), jnp.zeros((H, KA - KQ), f32)], axis=1)
    second_out = jnp.repeat(w_out.T, T, axis=0)
    second_in = jnp.repeat(w_in, T, axis=0)
    bias_col = jnp.repeat(bias_out, T)[:, None]

    field = pltpu.VMEM((Q, 2, rows + 2 * PAD, lanes), f32)
    vmem = pl.BlockSpec(memory_space=pltpu.VMEM)
    dma = pltpu.SemaphoreType.DMA
    grad_start, sums = pl.pallas_call(
        functools.partial(kernel, nx, ny, factor),
        out_shape=(
            jax.ShapeDtypeStruct(dist_start.shape, f32),
            jax.ShapeDtypeStruct((72, H), f32),
        ),
        in_specs=[vmem] * 8,
        out_specs=(vmem, vmem),
        scratch_shapes=[
            field,
            field,
            field,
            pltpu.VMEM((3, 2, rows, lanes), f32),
            pltpu.VMEM((3, 2, rows + 2 * PAD, lanes), f32),
            pltpu.VMEM((tiles, T * H, 2 * lanes), bf16),
            pltpu.VMEM((T * H, KA), bf16),
            pltpu.VMEM((T * H, KA), bf16),
            pltpu.VMEM((KQ, T * H), bf16),
            pltpu.VMEM((KQ, T * H), bf16),
            pltpu.VMEM((T * H, 2 * lanes), bf16),
            pltpu.VMEM((T * H, 2 * lanes), bf16),
            pltpu.VMEM((KA, T * H), f32),
            pltpu.VMEM((KA, T * H), f32),
            pltpu.VMEM((KQ, 2 * lanes), f32),
            pltpu.VMEM((72, H), f32),
            pltpu.VMEM((72, H), f32),
            pltpu.VMEM((nx, 72, H), f32),
            pltpu.VMEM((ny, 72, H), f32),
            dma((3, 8)),
            dma((3, 8)),
            dma((nx - 1,)),
            dma((nx - 1,)),
            dma((ny - 1,)),
            dma((ny - 1,)),
        ],
        compiler_params=pltpu.CompilerParams(
            collective_id=0, has_side_effects=True, vmem_limit_bytes=60 * 1024 * 1024
        ),
    )(dist_start, cotangent, solid_mask, first_in, first_out, second_out, second_in, bias_col)
    return (
        grad_start,
        sums[0:Q],
        sums[Q],
        sums[24 : 24 + Q].T,
        sums[48 : 48 + Q, 0],
    )


def solution(mesh):
    placed = (
        P(None, None, "gx", "gy"),
        P(None, None, "gx", "gy"),
        P(None, "gx", "gy"),
        P(),
        P(),
        P(),
        P(),
    )
    return jax.shard_map(
        shards,
        mesh=mesh,
        in_specs=placed,
        out_specs=(P(None, None, "gx", "gy"), P(), P(), P(), P()),
        check_vma=False,
    )
```

profile of v0, /device:TPU:1, one launch (start us, length us, event | category | flops | bytes accessed | tf_op | source)
XLA Modules:
  0.0 90.9 jit_solution(6516736201967488401)
XLA Ops:
  0.6 0.7 fusion.1
  1.3 0.1 copy.18
  1.4 0.1 copy.19
  1.5 0.1 copy.20
  1.6 0.7 fusion.2
  2.3 0.1 copy.17
  2.5 0.8 concatenate.6.first_in
  3.2 0.7 convert_bitcast_fusion
  3.9 0.7 broadcast_bitcast_fusion
  4.6 0.1 copy.21
  4.7 0.6 concatenate.7.first_out
  5.4 0.7 broadcast_in_dim.24
  6.1 0.7 broadcast_in_dim_reshape.4.bias_out
  6.8 76.8 %shard_map.110 = (f32[19,2,128,128]{3,2,1,0:T(8,128)}, f32[72,128]{1,0:T(8,128)}) custom-call(f32[19,2,128,128]{3,2,1,0:T(8,128)} %dist.1, f32[19,2,128,128]{3,2,1,0:T(8,128)} %cot.1, s32[2,128,128]{2,1,0:T(8,128)} %solid.1, f32[128,176]{1,0:T(8,128)} %concatenate.6.first_in, f32[128,176]{1,0:T(8,128)} %concatenate.7.first_out, ...), custom_call_target="tpu_custom_call" | custom-call | tf_op jit(solution)/shard_map/pallas_call | solution.py:367
  83.7 1.3 %slice_bitcast_fusion = (f32[128,19]{0,1:T(8,128)}, f32[19,128]{1,0:T(8,128)}) fusion(f32[72,128]{1,0:T(8,128)} %get-tuple-element.8), kind=kLoop, calls=%fused_computation.5 | loop fusion | bytes 38912 | tf_op jit(solution)/shard_map/transpose | solution.py:410
  85.0 1.2 %slice_bitcast_fusion.1 = f32[128]{0:T(128)} fusion(f32[72,128]{1,0:T(8,128)} %get-tuple-element.8), kind=kLoop, calls=%fused_computation.14 | loop fusion | bytes 1024 | tf_op jit(solution)/shard_map/squeeze | solution.py:409
  86.2 1.3 %slice_reduce_fusion = f32[19]{0:T(128)} fusion(f32[72,128]{1,0:T(8,128)} %get-tuple-element.8), kind=kLoop, calls=%fused_computation.4 | loop fusion | bytes 152 | tf_op jit(solution)/shard_map/slice | solution.py:411
  87.5 3.4 %copy.24 = f32[19,2,128,128]{3,2,1,0:T(8,128)} copy(f32[19,2,128,128]{3,2,1,0:T(8,128)} %get-tuple-element.25) | data formatting | bytes 4980736
  (3 shorter events, 0.0 us)
where the time goes:
time: 91.5 us; the launch traced here: 90.9 us
  Pallas kernels  76.8 us (84%)
  local copies, waits for them, and re-layouts  11.4 us (12%)
  other arithmetic  2.05 us (2%)
    pallas_call x1, Pallas kernels, shards(): pl.pallas_call(functools.partial(kernel, nx, ny, factor), out_shape=(jax....  76.8 us
    unnamed x1, local copies, waits for them, and re-layouts  3.43 us

commit v1 on v0

--- a/solution.py
+++ b/solution.py
@@ -56,13 +56,15 @@
     dist,
     cot,
     solid,
-    first_in,
-    first_out,
-    second_out,
-    second_in,
-    bias_out,
+    weight_in,
+    bias_in,
+    weight_out,
+    bias_row,
     grad_start,
-    sums,
+    grad_weight_in,
+    grad_bias_in,
+    grad_weight_out,
+    grad_bias_out,
     post_f,
     cot_f,
     mid_f,
@@ -78,6 +80,7 @@
     acc_in,
     acc_out,
     acc_bias,
+    bias_out,
     part_x,
     part_y,
     all_x,
@@ -92,7 +95,7 @@
     me_x, me_y = lax.axis_index("gx"), lax.axis_index("gy")
     rows = dist.shape[2]
     tiles = rows // T
-    H = first_in.shape[0]
+    H = weight_in.shape[1]
     lanes = dist.shape[3]
     right_x, left_x = lax.rem(me_x + 1, nx), lax.rem(me_x + nx - 1, nx)
     right_y, left_y = lax.rem(me_y + 1, ny), lax.rem(me_y + ny - 1, ny)
@@ -104,15 +107,33 @@
     for other in others:
         pl.semaphore_signal(barrier, inc=1, device_id=other, device_id_type=MESH)
 
+    ident = lax.broadcasted_iota(jnp.int32, (2 * H, Q), 0) >> 3
+    repeat = jnp.where(ident == lax.broadcasted_iota(jnp.int32, (2 * H, Q), 1), 1.0, 0.0)
+    spread = repeat.astype(jnp.bfloat16)
+    tall_in = jnp.dot(spread, weight_in[...], preferred_element_type=jnp.float32)
+    tall_out = lax.dot_general(
+        spread, weight_out[...], (((1,), (1,)), ((), ())), preferred_element_type=jnp.float32
+    )
+    second_in, second_out = tall_in[:KQ], tall_out[:KQ]
+    left = bias_in[...]
+    place = lax.broadcasted_iota(jnp.int32, (2 * H, H), 0)
+    for n in range(3):
+        addend = left.astype(jnp.bfloat16).astype(jnp.float32)
+        tall_in = jnp.where(place == KQ + n, addend, tall_in)
+        left = left - addend
+    first_in = jnp.transpose(tall_in)[:, :KA]
+    first_out = jnp.transpose(tall_out)[:, :KA]
+    column = jnp.sum(repeat[:KQ] * bias_row[...], axis=1, keepdims=True)
+    bias_out[...] = jnp.broadcast_to(column, bias_out.shape)
     col = lax.broadcasted_iota(jnp.int32, (H, KA), 1)
     row = lax.broadcasted_iota(jnp.int32, (KQ, H), 0)
     for s in range(T):
         keep = (col >= KQ) | ((col & (T - 1)) == s)
-        a_in[s * H : (s + 1) * H, :] = jnp.where(keep, first_in[...], 0.0).astype(jnp.bfloat16)
-        a_out[s * H : (s + 1) * H, :] = jnp.where(keep, first_out[...], 0.0).astype(jnp.bfloat16)
+        a_in[s * H : (s + 1) * H, :] = jnp.where(keep, first_in, 0.0).astype(jnp.bfloat16)
+        a_out[s * H : (s + 1) * H, :] = jnp.where(keep, first_out, 0.0).astype(jnp.bfloat16)
         mine = (row & (T - 1)) == s
-        b_out[:, s * H : (s + 1) * H] = jnp.where(mine, second_out[...], 0.0).astype(jnp.bfloat16)
-        b_in[:, s * H : (s + 1) * H] = jnp.where(mine, second_in[...], 0.0).astype(jnp.bfloat16)
+        b_out[:, s * H : (s + 1) * H] = jnp.where(mine, second_out, 0.0).astype(jnp.bfloat16)
+        b_in[:, s * H : (s + 1) * H] = jnp.where(mine, second_in, 0.0).astype(jnp.bfloat16)
     acc_in[...] = jnp.zeros_like(acc_in)
     acc_out[...] = jnp.zeros_like(acc_out)
     acc_bias[...] = jnp.zeros_like(acc_bias)
@@ -232,7 +253,7 @@
         put(post_f, 1, 1, i, posts)
         return carry
 
-    lax.fori_loop(0, tiles, collide, 0)
+    lax.fori_loop(0, tiles, collide, 0, unroll=2)
     second = copies(post_f, 1, 1)
     for copy in second:
         copy.start()
@@ -273,7 +294,7 @@
         put(mid_f, 2, -1, i, results)
         return carry
 
-    lax.fori_loop(0, tiles, late, 0)
+    lax.fori_loop(0, tiles, late, 0, unroll=2)
     third = copies(mid_f, 2, -1)
     for copy in third:
         copy.start()
@@ -294,7 +315,7 @@
                 grad_start[q, z, pl.ds(begin, T), :] = results[q][:, z * lanes : (z + 1) * lanes]
         return carry
 
-    lax.fori_loop(0, tiles, early, 0)
+    lax.fori_loop(0, tiles, early, 0, unroll=2)
 
     tall = lax.broadcasted_iota(jnp.int32, (KA, H), 0) & (T - 1)
 
@@ -305,8 +326,8 @@
         return jnp.sum(total.reshape(KA // T, T, H), axis=1)
 
     part_x[...] = jnp.zeros_like(part_x)
-    part_x[0 : KA // T, :] = diagonal(acc_in)
-    part_x[24 : 24 + KA // T, :] = diagonal(acc_out)
+    part_x[0 : KA // T, :] = diagonal(acc_out)
+    part_x[24 : 24 + KA // T, :] = diagonal(acc_in)
     bias = jnp.sum(acc_bias[...], axis=1, keepdims=True)
     bias = jnp.broadcast_to(bias, (KQ, H)).reshape(Q, T, H)
     part_x[48 : 48 + Q, :] = jnp.sum(bias, axis=1)
@@ -334,7 +355,15 @@
         return total
 
     part_y[...] = gather(part_x, all_x, nx, me_x, lambda a: (a, me_y), sx_sem, rx_sem)
-    sums[...] = gather(part_y, all_y, ny, me_y, lambda b: (me_x, b), sy_sem, ry_sem) * factor
+    sums = gather(part_y, all_y, ny, me_y, lambda b: (me_x, b), sy_sem, ry_sem) * factor
+    grad_weight_in[...] = sums[24 : 24 + Q]
+    grad_bias_in[...] = sums[24 + Q : 25 + Q]
+
+    def across(part):
+        return jnp.transpose(jnp.concatenate([part, jnp.zeros((H - 24, H), jnp.float32)], axis=0))
+
+    grad_weight_out[...] = across(sums[0:24])[:, :Q]
+    grad_bias_out[...] = across(sums[48:72])[0:1, :Q]
 
 
 def shards(dist_start, cotangent, solid_mask, weight_in, bias_in, weight_out, bias_out):
@@ -345,33 +374,20 @@
     f32, bf16 = jnp.float32, jnp.bfloat16
     factor = 1.0 / math.sqrt(solid_mask.size * nx * ny)
 
-    def top(x):
-        return lax.reduce_precision(x, 8, 7)
-
-    one = top(bias_in)
-    two = top(bias_in - one)
-    three = top(bias_in - one - two)
-    biases = jnp.stack([one, two, three], axis=1)
-    w_in, w_out = weight_in.astype(f32), weight_out.astype(f32)
-    first_in = jnp.concatenate(
-        [jnp.repeat(w_in.T, T, axis=1), biases, jnp.zeros((H, KA - KQ - 3), f32)], axis=1
-    )
-    first_out = jnp.concatenate([jnp.repeat(w_out, T, axis=1), jnp.zeros((H, KA - KQ), f32)], axis=1)
-    second_out = jnp.repeat(w_out.T, T, axis=0)
-    second_in = jnp.repeat(w_in, T, axis=0)
-    bias_col = jnp.repeat(bias_out, T)[:, None]
-
     field = pltpu.VMEM((Q, 2, rows + 2 * PAD, lanes), f32)
     vmem = pl.BlockSpec(memory_space=pltpu.VMEM)
     dma = pltpu.SemaphoreType.DMA
-    grad_start, sums = pl.pallas_call(
+    grad_start, d_weight_in, d_bias_in, d_weight_out, d_bias_out = pl.pallas_call(
         functools.partial(kernel, nx, ny, factor),
         out_shape=(
             jax.ShapeDtypeStruct(dist_start.shape, f32),
-            jax.ShapeDtypeStruct((72, H), f32),
+            jax.ShapeDtypeStruct((Q, H), f32),
+            jax.ShapeDtypeStruct((1, H), f32),
+            jax.ShapeDtypeStruct((H, Q), f32),
+            jax.ShapeDtypeStruct((1, Q), f32),
         ),
-        in_specs=[vmem] * 8,
-        out_specs=(vmem, vmem),
+        in_specs=[vmem] * 7,
+        out_specs=(vmem,) * 5,
         scratch_shapes=[
             field,
             field,
@@ -388,6 +404,7 @@
             pltpu.VMEM((KA, T * H), f32),
             pltpu.VMEM((KA, T * H), f32),
             pltpu.VMEM((KQ, 2 * lanes), f32),
+            pltpu.VMEM((KQ, 2 * lanes), f32),
             pltpu.VMEM((72, H), f32),
             pltpu.VMEM((72, H), f32),
             pltpu.VMEM((nx, 72, H), f32),
@@ -402,14 +419,8 @@
         compiler_params=pltpu.CompilerParams(
             collective_id=0, has_side_effects=True, vmem_limit_bytes=60 * 1024 * 1024
         ),
-    )(dist_start, cotangent, solid_mask, first_in, first_out, second_out, second_in, bias_col)
-    return (
-        grad_start,
-        sums[0:Q],
-        sums[Q],
-        sums[24 : 24 + Q].T,
-        sums[48 : 48 + Q, 0],
-    )
+    )(dist_start, cotangent, solid_mask, weight_in, bias_in[None], weight_out, bias_out[None])
+    return grad_start, d_weight_in, d_bias_in[0], d_weight_out, d_bias_out[0]
 
 
 def solution(mesh):

time: 91.5 us -> 78.4 us (0.86)
  Pallas kernels: 76.8 us -> 69.5 us
  local copies, waits for them, and re-layouts: 11.4 us -> 8.01 us
  other arithmetic: 2.05 us -> 0 us
    pallas_call x1, Pallas kernels: 76.8 us -> 69.5 us  [shards(): pl.pallas_call(functools.partial(kernel, nx, ny, factor), out_shape=(jax....]
    unnamed x1 -> x12, local copies, waits for them, and re-layouts: 3.43 us -> 8.01 us
    concatenate x2 -> x0, local copies, waits for them, and re-layouts: 1.44 us -> none  [the longest x1 0.79 us: shards(): jnp.concatenate([jnp.repeat(w_in.T, T, axis=1), biases, jnp.zeros((H, KA...]
    slice x1 -> x0, local copies, waits for them, and re-layouts: 1.33 us -> none  [shards(): sums[48:48 + Q, 0]]
    transpose x1 -> x0, local copies, waits for them, and re-layouts: 1.33 us -> none  [shards(): sums[24:24 + Q]]
    squeeze x1 -> x0, local copies, waits for them, and re-layouts: 1.19 us -> none  [shards(): sums[Q]]
    another operation x4 -> x0, local copies, waits for them, and re-layouts: 1.05 us -> none  [the longest x1 0.71 us: shards(): bias_col = jnp.repeat(bias_out, T)[:, None]]
where the time goes in v1:
time: 78.4 us; the launch traced here: 78.2 us
  Pallas kernels  69.5 us (89%)
  local copies, waits for them, and re-layouts  8.01 us (10%)
    pallas_call x1, Pallas kernels, shards(): pl.pallas_call(functools.partial(kernel, nx, ny, factor), out_shape=(jax....  69.5 us
    unnamed x12, local copies, waits for them, and re-layouts  8.01 us

profile of v1, /device:TPU:1, one launch (start us, length us, event | category | flops | bytes accessed | tf_op | source)
XLA Modules:
  0.0 78.2 jit_solution(10077912476956127364)
XLA Ops:
  0.6 1.4 %copy.12.weight_out = bf16[128,19]{1,0:T(8,128)(2,1)} copy(bf16[128,19]{0,1:T(8,128)(2,1)} %param.12) | data formatting | bytes 9728 | tf_op args[5]
  2.0 69.5 %shard_map.110 = (f32[19,2,128,128]{3,2,1,0:T(8,128)}, f32[19,128]{1,0:T(8,128)}, f32[1,128]{1,0:T(1,128)}, f32[128,19]{1,0:T(8,128)}, f32[1,19]{1,0:T(1,128)}) custom-call(f32[19,2,128,128]{3,2,1,0:T(8,128)} %dist.1, f32[19,2,128,128]{3,2,1,0:T(8,128)} %cot.1, s32[2,128,128]{2,1,0:T(8,128)} %solid.1, bf16[19,128]{1,0:T(8,128)(2,1)} %weight_in.1, ...), custom_call_target="tpu_custom_call" | custom-call | tf_op jit(solution)/shard_map/pallas_call | solution.py:380
  71.6 1.5 %copy.13 = f32[128,19]{0,1:T(8,128)} copy(f32[128,19]{1,0:T(8,128)} %get-tuple-element.18) | data formatting | bytes 19456
  73.1 0.0 copy-start
  73.1 0.0 copy-start.2
  73.1 0.0 copy-start.1
  73.1 3.4 %copy.18 = f32[19,2,128,128]{3,2,1,0:T(8,128)} copy(f32[19,2,128,128]{3,2,1,0:T(8,128)} %get-tuple-element.25) | data formatting | bytes 4980736
  76.6 0.0 copy-done
  76.6 0.6 copy.19
  77.2 0.0 copy-done.2
  77.2 0.5 copy.20
  77.7 0.0 copy-done.1
  77.7 0.5 copy.21
Async XLA Ops:
  73.1 3.5 %copy-start = (f32[19,128]{1,0:T(8,128)S(1)}, f32[19,128]{1,0:T(8,128)}, u32[]{:S(2)}) copy-start(f32[19,128]{1,0:T(8,128)} %get-tuple-element.26) | copy-start | bytes 29188
  73.1 4.1 %copy-start.2 = (f32[1,128]{1,0:T(1,128)S(1)}, f32[1,128]{1,0:T(1,128)}, u32[]{:S(2)}) copy-start(f32[1,128]{1,0:T(1,128)} %get-tuple-element.12) | copy-start | bytes 1540
  73.1 4.6 %copy-start.1 = (f32[1,19]{1,0:T(1,128)S(1)}, f32[1,19]{1,0:T(1,128)}, u32[]{:S(2)}) copy-start(f32[1,19]{1,0:T(1,128)} %get-tuple-element.14) | copy-start | bytes 232
